TPU v7x, 32 devices: a whole 2x2x4 slice. The times are simulated.
32 devices in a mesh: parts: 2 (over x), seq: 16 (over z, y, core).
Axes of the slice: x: 2, y: 2, z: 4, core: 2. Of those that a mesh axis runs over, the one named last changes fastest.
Arguments:
- prefix_latent: bfloat16 [61440, 512], P(('parts', 'seq')), parts along dimension 0, may hold values from -6 to 6
- block_order: int32 [480], P(('parts', 'seq')), parts along dimension 0, may hold values from 0 to 239, each once
- key_up: bfloat16 [512, 512], replicated, may hold values from -0.25 to 0.25
- value_up: bfloat16 [512, 512], replicated, may hold values from -0.25 to 0.25
- queries: bfloat16 [32, 4, 4096], P(('parts', 'seq')), parts along dimension 0, may hold values from -200 to 200
- new_keys: bfloat16 [32, 4, 512], P(('parts', 'seq')), parts along dimension 0, may hold values from -6 to 6
- new_values: bfloat16 [32, 4, 512], P(('parts', 'seq')), parts along dimension 0, may hold values from -6 to 6
- suffix_keys: bfloat16 [32, 4096, 512], P(('parts', 'seq')), parts along dimension 0, may hold values from -6 to 6
- suffix_values: bfloat16 [32, 4096, 512], P(('parts', 'seq')), parts along dimension 0, may hold values from -6 to 6
- suffix_len: int32 [32], P(('parts', 'seq')), parts along dimension 0, may hold values from 1 to 4096, 32768 in all
Outputs:
- attended: bfloat16 [32, 4, 4096], P(('parts', 'seq')), parts along dimension 0
There are 2 independent parts, one for each index of `parts`. A program takes and returns all parts, laid end to end along the dimension named above; an argument that names none is the same for every part. Nothing has to cross between parts.
Inputs may be any that keep to these rules, and one draw needn't show every extreme that they name: A request's cache holds its first suffix_len entries; some request holds exactly 4096. `block_order`: each block position appears once.
All inputs are finite; a program needn't handle non-finite values. No bound on the sum of `suffix_len` on one device may be relied on, other than what follows from the above.
Results may differ from a plain program's by a relative error of at most 0.005.
The roundings to bfloat16 on the way count: a program that leaves them out, or rounds other values in their place, can miss the bound.
Values may be sent and summed in bfloat16 or wider, within the bound.
No kernel may reach another device: no remote copies, remote signals or barrier semaphores. Data moves between devices by JAX's collectives and lax.ppermute only.
A program may use at most 128 MiB of HBM per device.

v0:
```python
import math
import jax
import jax.numpy as jnp
import numpy as np
from jax import lax
from jax.sharding import PartitionSpec as P

HD = 128
QH = 32
KVH = 4
BLK = 128
STEPS = 4
SUF = 4096


def phase_table(half):
    index = np.arange(half)
    freq = 500000.0 ** (-2.0 * index / (2 * half))
    mult = np.floor(2.0**24 * freq / (2 * np.pi)).astype(np.int64)
    return ((mult >> 12).astype(np.int32), (mult & 4095).astype(np.int32))


def rotate(values, position):
    half = values.shape[-1] // 2
    high, low = phase_table(half)
    spot = position[..., None]
    first = spot * jnp.asarray(low, dtype=jnp.int32)
    second = spot * jnp.asarray(high, dtype=jnp.int32) % 4096
    turns = (first + second * 4096) % 16777216
    angle = turns.astype(values.dtype) * (2.0 * math.pi / 16777216.0)
    cosine = jnp.cos(angle)[..., None, :]
    sine = jnp.sin(angle)[..., None, :]
    lower = values[..., :half]
    upper = values[..., half:]
    return jnp.concatenate([lower * cosine - upper * sine, upper * cosine + lower * sine], -1)


def local(
    prefix_latent,
    block_order,
    key_up,
    value_up,
    queries,
    new_keys,
    new_values,
    suffix_keys,
    suffix_values,
    suffix_len,
):
    seq_count = lax.axis_size("seq")
    pre_rows = prefix_latent.shape[0]
    prefix = pre_rows * seq_count
    req_rows = queries.shape[0]
    group = QH // KVH
    scale = 1.0 / math.sqrt(HD)
    rows = jnp.arange(pre_rows, dtype=jnp.int32)
    key_pos = jnp.repeat(block_order, BLK) * BLK + rows % BLK
    keys = jnp.dot(prefix_latent, key_up, preferred_element_type=jnp.float32).reshape(
        pre_rows, KVH, HD
    )
    keys = rotate(keys, key_pos).astype(jnp.bfloat16)
    values = (
        jnp.dot(prefix_latent, value_up, preferred_element_type=jnp.float32)
        .astype(jnp.bfloat16)
        .reshape(pre_rows, KVH, HD)
    )
    step_index = jnp.arange(STEPS, dtype=jnp.int32)
    query_pos = prefix + suffix_len[:, None] + step_index[None, :]
    query_rot = rotate(
        queries.astype(jnp.float32).reshape(req_rows, STEPS, QH, HD), query_pos
    ).astype(jnp.bfloat16)
    new_rot = rotate(
        new_keys.astype(jnp.float32).reshape(req_rows, STEPS, KVH, HD), query_pos
    ).astype(jnp.bfloat16)

    def shard_part(query_block):
        count = query_block.shape[0]
        width = query_block.shape[1]
        split = query_block.reshape(count, width, KVH, group, HD)
        scores = (
            jnp.einsum("rtkgd,pkd->rtkgp", split, keys, preferred_element_type=jnp.float32) * scale
        )
        peak = jnp.max(scores, -1)
        expo = jnp.exp(scores - peak[..., None])
        total = jnp.sum(expo, -1)
        summed = jnp.einsum(
            "rtkgp,pkd->rtkgd",
            expo.astype(jnp.bfloat16),
            values,
            preferred_element_type=jnp.float32,
        )
        part = summed / total[..., None]
        return (
            part.reshape(count, width, QH * HD),
            peak.reshape(count, width, QH),
            total.reshape(count, width, QH),
        )

    def prefix_attention(selected):
        width = selected.shape[1]
        whole = lax.all_gather(selected, "seq", axis=0, tiled=True)
        count = whole.shape[0]
        per_block = math.gcd(count, max(1, 512 // (width * QH)))
        blocks = whole.reshape(count // per_block, per_block, width, QH * HD)
        parts, peaks, totals = lax.map(shard_part, blocks)
        parts = parts.reshape(count, width, QH * HD)
        peaks = peaks.reshape(count, width, QH)
        totals = totals.reshape(count, width, QH)
        got_parts, got_peaks, got_totals = (
            lax.all_to_all(parts[:, None], "seq", split_axis=0, concat_axis=1, tiled=True),
            lax.all_to_all(peaks[:, None], "seq", split_axis=0, concat_axis=1, tiled=True),
            lax.all_to_all(totals[:, None], "seq", split_axis=0, concat_axis=1, tiled=True),
        )
        highest = jnp.max(got_peaks, 1)
        factor = got_totals * jnp.exp(got_peaks - highest[:, None])
        numer = jnp.sum(
            factor[..., None] * got_parts.reshape(req_rows, seq_count, width, QH, HD), 1
        )
        denom = jnp.sum(factor, 1)
        return (highest, numer, denom)

    flat_queries = query_rot.reshape(req_rows, STEPS, QH * HD)
    results = [prefix_attention(flat_queries[:, which : which + 1]) for which in range(STEPS)]
    highest = jnp.concatenate([entry[0] for entry in results], 1)
    numer = jnp.concatenate([entry[1] for entry in results], 1)
    denom = jnp.concatenate([entry[2] for entry in results], 1)
    split = query_rot.reshape(req_rows, STEPS, KVH, group, HD)
    cache_keys = suffix_keys.reshape(req_rows, SUF, KVH, HD)
    cache_values = suffix_values.reshape(req_rows, SUF, KVH, HD)
    cache_scores = (
        jnp.einsum("rtkgd,rpkd->rtkgp", split, cache_keys, preferred_element_type=jnp.float32)
        * scale
    )
    live = jnp.arange(SUF, dtype=jnp.int32)[None, :] < suffix_len[:, None]
    cache_scores = jnp.where(live[:, None, None, None, :], cache_scores, -jnp.inf)
    fresh_keys = new_rot.reshape(req_rows, STEPS, KVH, HD)
    fresh_values = new_values.reshape(req_rows, STEPS, KVH, HD)
    fresh_scores = (
        jnp.einsum("rtkgd,rukd->rtkgu", split, fresh_keys, preferred_element_type=jnp.float32)
        * scale
    )
    causal = step_index[:, None] >= step_index[None, :]
    fresh_scores = jnp.where(causal[None, :, None, None, :], fresh_scores, -jnp.inf)
    local_peak = jnp.maximum(jnp.max(cache_scores, -1), jnp.max(fresh_scores, -1))
    cache_exp = jnp.exp(cache_scores - local_peak[..., None])
    fresh_exp = jnp.exp(fresh_scores - local_peak[..., None])
    local_total = jnp.sum(cache_exp, -1) + jnp.sum(fresh_exp, -1)
    local_numer = jnp.einsum(
        "rtkgp,rpkd->rtkgd",
        cache_exp.astype(jnp.bfloat16),
        cache_values,
        preferred_element_type=jnp.float32,
    )
    local_numer = local_numer + jnp.einsum(
        "rtkgu,rukd->rtkgd",
        fresh_exp.astype(jnp.bfloat16),
        fresh_values,
        preferred_element_type=jnp.float32,
    )
    local_peak = local_peak.reshape(req_rows, STEPS, QH)
    local_total = local_total.reshape(req_rows, STEPS, QH)
    local_numer = local_numer.reshape(req_rows, STEPS, QH, HD)
    biggest = jnp.maximum(highest, local_peak)
    prefix_weight = jnp.exp(highest - biggest)
    local_weight = jnp.exp(local_peak - biggest)
    result = (numer * prefix_weight[..., None] + local_numer * local_weight[..., None]) / (
        denom * prefix_weight + local_total * local_weight
    )[..., None]
    return result.reshape(req_rows, STEPS, QH * HD).astype(jnp.bfloat16)


def solution(mesh):
    placed = (
        P(("parts", "seq"), None),
        P(("parts", "seq")),
        P(),
        P(),
        P(("parts", "seq"), None, None),
        P(("parts", "seq"), None, None),
        P(("parts", "seq"), None, None),
        P(("parts", "seq"), None, None),
        P(("parts", "seq"), None, None),
        P(("parts", "seq")),
    )
    return jax.shard_map(
        local,
        mesh=mesh,
        in_specs=placed,
        out_specs=P(("parts", "seq"), None, None),
        check_vma=False,
    )
```

profile of v0, /device:TPU:0, one launch (start us, length us, event | category | flops | bytes accessed | tf_op | source)
XLA Modules:
  0.0 271.2 jit_solution(17228398530204130083)
XLA Ops:
  3.2 23.8 %all_gather.12 = bf16[16,1,4096]{2,1,0:T(2,128)(2,1)S(1)} all-gather(bf16[1,1,4096]{2,1,0:T(2,128)(2,1)S(1)} %get-tuple-element.75), channel_id=1, replica_groups=mesh['parts'=2,'seq'=16] {'seq'}, dimensions={0}, use_global_device_ids=true | all-gather | bytes 139264 | tf_op jit(solution)/shard_map/all_gather | solution.py:101
  32.5 3.7 %copy.155 = f32[1920,4,64]{2,0,1:T(8,128)} copy(f32[1920,4,64]{0,2,1:T(8,128)} %get-tuple-element.72) | data formatting | bytes 3932160
  36.1 3.7 %copy.156 = f32[1920,4,64]{2,0,1:T(8,128)} copy(f32[1920,4,64]{0,2,1:T(8,128)} %get-tuple-element.71) | data formatting | bytes 3932160
  39.9 4.3 %fusion.77 = (f32[1920,64]{1,0:T(8,128)S(1)}, f32[1920,64]{1,0:T(8,128)S(1)}) fusion(s32[64]{0:T(128)S(1)} %copy-done.20, s32[64]{0:T(128)S(1)} %copy-done.19, s32[1920]{0:T(1024)S(1)} %fusion.96), kind=kLoop, calls=%fused_computation.80 | loop fusion | flops 3440640 | bytes 991232 | tf_op jit(solution)/shard_map/cos | solution.py:31
  44.3 4.5 %subtract_convert_fusion = (bf16[1920,4,64]{2,0,1:T(8,128)(2,1)S(1)}, bf16[1920,4,64]{2,0,1:T(8,128)(2,1)S(1)}) fusion(f32[1920,4,64]{2,0,1:T(8,128)} %copy.156, f32[1920,4,64]{2,0,1:T(8,128)} %copy.155, f32[1920,64]{1,0:T(8,128)S(1)} %get-tuple-element.89, f32[1920,64]{1,0:T(8,128)S(1)} %get-tuple-element.88), kind=kLoop, calls=%fused_computation.20 | loop fusion | flops 3932160 | bytes 6881280 | tf_op jit(solution)/shard_map/convert.12
  54.4 3.7 %all-to-all-start = ((f32[16,1,1,32]{3,2,1,0:T(1,128)}), f32[16,1,1,32]{3,2,1,0:T(1,128)S(1)}, u32[]{:S(2)}, u32[]{:S(2)}) async-start(f32[16,1,1,32]{3,2,1,0:T(1,128)} %copy.101), calls=%async_computation | async-start | bytes 16384 | tf_op jit(solution)/shard_map/all_to_all | solution.py:112
  61.1 22.2 %all_gather.13 = bf16[16,1,4096]{2,1,0:T(2,128)(2,1)S(1)} all-gather(bf16[1,1,4096]{2,1,0:T(2,128)(2,1)S(1)} %get-tuple-element.85), channel_id=1, replica_groups=mesh['parts'=2,'seq'=16] {'seq'}, dimensions={0}, use_global_device_ids=true | all-gather | bytes 139264 | tf_op jit(solution)/shard_map/all_gather | solution.py:101
  87.2 18.2 %all_gather.14 = bf16[16,1,4096]{2,1,0:T(2,128)(2,1)S(1)} all-gather(bf16[1,1,4096]{2,1,0:T(2,128)(2,1)S(1)} %get-tuple-element.84), channel_id=1, replica_groups=mesh['parts'=2,'seq'=16] {'seq'}, dimensions={0}, use_global_device_ids=true | all-gather | bytes 139264 | tf_op jit(solution)/shard_map/all_gather | solution.py:101
  109.4 19.5 %all_gather.15 = bf16[16,1,4096]{2,1,0:T(2,128)(2,1)S(1)} all-gather(bf16[1,1,4096]{2,1,0:T(2,128)(2,1)S(1)} %get-tuple-element.76), channel_id=1, replica_groups=mesh['parts'=2,'seq'=16] {'seq'}, dimensions={0}, use_global_device_ids=true | all-gather | bytes 139264 | tf_op jit(solution)/shard_map/all_gather | solution.py:101
  133.5 6.9 %reshape.1695 = bf16[4096,4,128]{2,1,0:T(4,128)(2,1)} reshape(bf16[1,4096,512]{2,1,0:T(8,128)(2,1)} %param.23) | data formatting | bytes 8388608 | tf_op jit(solution)/shard_map/reshape.165
  140.4 3.8 %all-to-all-start.1 = ((f32[16,1,1,32]{3,2,1,0:T(1,128)}), f32[16,1,1,32]{3,2,1,0:T(1,128)S(1)}, u32[]{:S(2)}, u32[]{:S(2)}) async-start(f32[16,1,1,32]{3,2,1,0:T(1,128)} %copy.102), calls=%async_computation.1 | async-start | bytes 16384 | tf_op jit(solution)/shard_map/all_to_all | solution.py:111
  144.2 3.8 %fusion.125 = (f32[4,4,8]{2,0,1:T(4,128)S(1)}, f32[1,4,4,8,4096]{4,3,1,2,0:T(8,128)S(1)}) fusion(bf16[4096,4,128,1]{2,1,0,3:T(4,128)(2,1)} %bitcast.286, pred[4096]{0:T(1024)(128)(4,1)S(1)} %iota_compare_fusion, bf16[4,4,8,64]{3,2,1,0:T(8,128)(2,1)S(1)} %bitcast.301, bf16[4,4,8,64]{3,2,1,0:T(8,128)(2,1)S(1)} %bitcast.299), kind=kOutput, calls=%fused_computation.167 | convolution fusion | flops 135856000 | bytes 6328832 | tf_op jit(solution)/shard_map/rtkgd,rpkd->rtkgp/dot_general | solution.py:131
  150.6 4.1 %all-to-all-start.3 = ((f32[16,1,1,32]{3,2,1,0:T(1,128)}), f32[16,1,1,32]{3,2,1,0:T(1,128)S(1)}, u32[]{:S(2)}, u32[]{:S(2)}) async-start(f32[16,1,1,32]{3,2,1,0:T(1,128)} %copy.107), calls=%async_computation.3 | async-start | bytes 16384 | tf_op jit(solution)/shard_map/all_to_all | solution.py:112
  155.4 5.6 %all-to-all-done.3 = f32[16,1,1,32]{3,2,1,0:T(1,128)S(1)} async-done(((f32[16,1,1,32]{3,2,1,0:T(1,128)}), f32[16,1,1,32]{3,2,1,0:T(1,128)S(1)}, u32[]{:S(2)}, u32[]{:S(2)}) %all-to-all-start.3) | async-done | bytes 2080 | tf_op jit(solution)/shard_map/all_to_all | solution.py:112
  161.0 3.5 %all-to-all-start.4 = ((f32[16,1,1,32]{3,2,1,0:T(1,128)}), f32[16,1,1,32]{3,2,1,0:T(1,128)S(1)}, u32[]{:S(2)}, u32[]{:S(2)}) async-start(f32[16,1,1,32]{3,2,1,0:T(1,128)} %copy.108), calls=%async_computation.4 | async-start | bytes 16384 | tf_op jit(solution)/shard_map/all_to_all | solution.py:111
  165.3 5.6 %all-to-all-done.4 = f32[16,1,1,32]{3,2,1,0:T(1,128)S(1)} async-done(((f32[16,1,1,32]{3,2,1,0:T(1,128)}), f32[16,1,1,32]{3,2,1,0:T(1,128)S(1)}, u32[]{:S(2)}, u32[]{:S(2)}) %all-to-all-start.4) | async-done | bytes 2080 | tf_op jit(solution)/shard_map/all_to_all | solution.py:111
  170.9 3.5 %all-to-all-start.6 = ((f32[16,1,1,32]{3,2,1,0:T(1,128)}), f32[16,1,1,32]{3,2,1,0:T(1,128)S(1)}, u32[]{:S(2)}, u32[]{:S(2)}) async-start(f32[16,1,1,32]{3,2,1,0:T(1,128)} %copy.113), calls=%async_computation.6 | async-start | bytes 16384 | tf_op jit(solution)/shard_map/all_to_all | solution.py:112
  175.1 5.6 %all-to-all-done.6 = f32[16,1,1,32]{3,2,1,0:T(1,128)S(1)} async-done(((f32[16,1,1,32]{3,2,1,0:T(1,128)}), f32[16,1,1,32]{3,2,1,0:T(1,128)S(1)}, u32[]{:S(2)}, u32[]{:S(2)}) %all-to-all-start.6) | async-done | bytes 2080 | tf_op jit(solution)/shard_map/all_to_all | solution.py:112
  181.3 3.5 %all-to-all-start.7 = ((f32[16,1,1,32]{3,2,1,0:T(1,128)}), f32[16,1,1,32]{3,2,1,0:T(1,128)S(1)}, u32[]{:S(2)}, u32[]{:S(2)}) async-start(f32[16,1,1,32]{3,2,1,0:T(1,128)} %copy.114), calls=%async_computation.7 | async-start | bytes 16384 | tf_op jit(solution)/shard_map/all_to_all | solution.py:111
  185.8 6.9 %reshape.1699 = bf16[4096,4,128]{2,1,0:T(4,128)(2,1)} reshape(bf16[1,4096,512]{2,1,0:T(8,128)(2,1)} %param.24) | data formatting | bytes 8388608 | tf_op jit(solution)/shard_map/reshape.180
  192.7 6.0 %all-to-all-start.9 = ((f32[16,1,1,32]{3,2,1,0:T(1,128)}), f32[16,1,1,32]{3,2,1,0:T(1,128)S(1)}, u32[]{:S(2)}, u32[]{:S(2)}) async-start(f32[16,1,1,32]{3,2,1,0:T(1,128)} %copy.119), calls=%async_computation.9 | async-start | bytes 16384 | tf_op jit(solution)/shard_map/all_to_all | solution.py:112
  198.7 3.0 %fusion.3 = f32[4,4,8,128]{3,2,1,0:T(8,128)S(1)} fusion(bf16[4096,4,128,1]{2,1,0,3:T(4,128)(2,1)} %bitcast.285, f32[1,4,4,8,4096]{4,3,1,2,0:T(8,128)S(1)} %get-tuple-element.117, f32[4,4,8]{2,0,1:T(4,128)S(1)} %max.48), kind=kOutput, calls=%fused_computation.4 | convolution fusion | flops 135266304 | bytes 6357504 | tf_op jit(solution)/shard_map/rtkgp,rpkd->rtkgd/dot_general | solution.py:148
  205.7 3.5 %all-to-all-start.10 = ((f32[16,1,1,32]{3,2,1,0:T(1,128)}), f32[16,1,1,32]{3,2,1,0:T(1,128)S(1)}, u32[]{:S(2)}, u32[]{:S(2)}) async-start(f32[16,1,1,32]{3,2,1,0:T(1,128)} %copy.120), calls=%async_computation.10 | async-start | bytes 16384 | tf_op jit(solution)/shard_map/all_to_all | solution.py:111
  210.4 5.1 %all-to-all-done.10 = f32[16,1,1,32]{3,2,1,0:T(1,128)S(1)} async-done(((f32[16,1,1,32]{3,2,1,0:T(1,128)}), f32[16,1,1,32]{3,2,1,0:T(1,128)S(1)}, u32[]{:S(2)}, u32[]{:S(2)}) %all-to-all-start.10) | async-done | bytes 2080 | tf_op jit(solution)/shard_map/all_to_all | solution.py:111
  215.5 3.5 %all-to-all-start.2 = ((f32[16,1,1,4096]{3,1,2,0:T(1,128)}), f32[16,1,1,4096]{3,1,2,0:T(1,128)S(1)}, u32[]{:S(2)}, u32[]{:S(2)}) async-start(f32[16,1,1,4096]{3,1,2,0:T(1,128)} %bitcast.19), calls=%async_computation.2 | async-start | bytes 524288 | tf_op jit(solution)/shard_map/all_to_all | solution.py:110
  222.1 7.0 %all-to-all-done.2 = f32[16,1,1,4096]{3,1,2,0:T(1,128)S(1)} async-done(((f32[16,1,1,4096]{3,1,2,0:T(1,128)}), f32[16,1,1,4096]{3,1,2,0:T(1,128)S(1)}, u32[]{:S(2)}, u32[]{:S(2)}) %all-to-all-start.2) | async-done | bytes 262176 | tf_op jit(solution)/shard_map/all_to_all | solution.py:110
  229.1 3.5 %all-to-all-start.5 = ((f32[16,1,1,4096]{3,1,2,0:T(1,128)}), f32[16,1,1,4096]{3,1,2,0:T(1,128)S(1)}, u32[]{:S(2)}, u32[]{:S(2)}) async-start(f32[16,1,1,4096]{3,1,2,0:T(1,128)} %bitcast.35), calls=%async_computation.5 | async-start | bytes 524288 | tf_op jit(solution)/shard_map/all_to_all | solution.py:110
  233.4 9.3 %all-to-all-done.5 = f32[16,1,1,4096]{3,1,2,0:T(1,128)S(1)} async-done(((f32[16,1,1,4096]{3,1,2,0:T(1,128)}), f32[16,1,1,4096]{3,1,2,0:T(1,128)S(1)}, u32[]{:S(2)}, u32[]{:S(2)}) %all-to-all-start.5) | async-done | bytes 262176 | tf_op jit(solution)/shard_map/all_to_all | solution.py:110
  242.6 3.5 %all-to-all-start.8 = ((f32[16,1,1,4096]{3,1,2,0:T(1,128)}), f32[16,1,1,4096]{3,1,2,0:T(1,128)S(1)}, u32[]{:S(2)}, u32[]{:S(2)}) async-start(f32[16,1,1,4096]{3,1,2,0:T(1,128)} %bitcast.50), calls=%async_computation.8 | async-start | bytes 524288 | tf_op jit(solution)/shard_map/all_to_all | solution.py:110
  247.6 8.6 %all-to-all-done.8 = f32[16,1,1,4096]{3,1,2,0:T(1,128)S(1)} async-done(((f32[16,1,1,4096]{3,1,2,0:T(1,128)}), f32[16,1,1,4096]{3,1,2,0:T(1,128)S(1)}, u32[]{:S(2)}, u32[]{:S(2)}) %all-to-all-start.8) | async-done | bytes 262176 | tf_op jit(solution)/shard_map/all_to_all | solution.py:110
  256.2 3.5 %all-to-all-start.11 = ((f32[16,1,1,4096]{3,1,2,0:T(1,128)}), f32[16,1,1,4096]{3,1,2,0:T(1,128)S(1)}, u32[]{:S(2)}, u32[]{:S(2)}) async-start(f32[16,1,1,4096]{3,1,2,0:T(1,128)} %bitcast.65), calls=%async_computation.11 | async-start | bytes 524288 | tf_op jit(solution)/shard_map/all_to_all | solution.py:110
  261.0 8.7 %all-to-all-done.11 = f32[16,1,1,4096]{3,1,2,0:T(1,128)S(1)} async-done(((f32[16,1,1,4096]{3,1,2,0:T(1,128)}), f32[16,1,1,4096]{3,1,2,0:T(1,128)S(1)}, u32[]{:S(2)}, u32[]{:S(2)}) %all-to-all-start.11) | async-done | bytes 262176 | tf_op jit(solution)/shard_map/all_to_all | solution.py:110
  (145 shorter events, 48.3 us)
Async XLA Ops:
  0.0 27.7 %copy-start = (bf16[1920,512]{1,0:T(8,128)(2,1)S(1)}, bf16[1920,512]{1,0:T(8,128)(2,1)}, u32[]{:S(2)}) copy-start(bf16[1920,512]{1,0:T(8,128)(2,1)} %param.16) | copy-start | bytes 5898244
  36.1 3.7 %copy-start.22 = (s32[15]{0:T(128)S(1)}, s32[15]{0:T(128)}, u32[]{:S(2)}) copy-start(s32[15]{0:T(128)} %param.17) | copy-start | bytes 184
  36.1 3.8 %copy-start.19 = (s32[64]{0:T(128)S(1)}, s32[64]{0:T(128)}, u32[]{:S(2)}) copy-start(s32[64]{0:T(128)} %constant.146.clone) | copy-start | bytes 772
  36.1 3.8 %copy-start.20 = (s32[64]{0:T(128)S(1)}, s32[64]{0:T(128)}, u32[]{:S(2)}) copy-start(s32[64]{0:T(128)} %constant.147.clone) | copy-start | bytes 772
  51.1 1.9 copy-start.4
  51.1 7.0 %copy-start.21 = (bf16[512,512]{1,0:T(8,128)(2,1)S(1)}, bf16[512,512]{1,0:T(8,128)(2,1)}, u32[]{:S(2)}) copy-start(bf16[512,512]{1,0:T(8,128)(2,1)} %param.19) | copy-start | bytes 1572868
  54.4 86.0 %all-to-all-start = ((f32[16,1,1,32]{3,2,1,0:T(1,128)}), f32[16,1,1,32]{3,2,1,0:T(1,128)S(1)}, u32[]{:S(2)}, u32[]{:S(2)}) async-start(f32[16,1,1,32]{3,2,1,0:T(1,128)} %copy.101), calls=%async_computation | async-start | bytes 16384 | tf_op jit(solution)/shard_map/all_to_all | solution.py:112
  58.1 2.1 copy-start.5
  59.4 1.7 copy-start.23
  59.4 24.6 %copy-start.3 = (bf16[1920,4,128,1]{2,0,3,1:T(8,128)(2,1)S(1)}, bf16[1920,4,128,1]{2,0,3,1:T(8,128)(2,1)}, u32[]{:S(2)}) copy-start(bf16[1920,4,128,1]{2,0,3,1:T(8,128)(2,1)} %copy-done.2) | copy-start | bytes 5898244
  84.8 1.5 copy-start.24
  86.4 20.6 %copy-start.11 = (f32[16,4,8]{0,2,1:T(8,128)}, f32[16,4,8]{0,2,1:T(8,128)S(1)}, u32[]{:S(2)}) copy-start(f32[16,4,8]{0,2,1:T(8,128)S(1)} %fusion.13) | copy-start | bytes 6148
  140.4 7.6 %copy-start.12 = (f32[16,4,8]{0,2,1:T(8,128)S(1)}, f32[16,4,8]{0,2,1:T(8,128)}, u32[]{:S(2)}) copy-start(f32[16,4,8]{0,2,1:T(8,128)} %copy-done.11) | copy-start | bytes 6148
  140.4 14.3 %copy-start.17 = (bf16[1,4,512]{2,1,0:T(4,128)(2,1)S(1)}, bf16[1,4,512]{2,1,0:T(4,128)(2,1)}, u32[]{:S(2)}) copy-start(bf16[1,4,512]{2,1,0:T(4,128)(2,1)} %param.21) | copy-start | bytes 12292
  140.4 24.1 %copy-start.14 = (f32[4,64]{1,0:T(4,128)S(1)}, f32[4,64]{1,0:T(4,128)}, u32[]{:S(2)}) copy-start(f32[4,64]{1,0:T(4,128)} %copy-done.13) | copy-start | bytes 3076
  140.4 24.1 %copy-start.16 = (f32[4,64]{1,0:T(4,128)S(1)}, f32[4,64]{1,0:T(4,128)}, u32[]{:S(2)}) copy-start(f32[4,64]{1,0:T(4,128)} %copy-done.15) | copy-start | bytes 3076
  140.4 10.2 %all-to-all-start.1 = ((f32[16,1,1,32]{3,2,1,0:T(1,128)}), f32[16,1,1,32]{3,2,1,0:T(1,128)S(1)}, u32[]{:S(2)}, u32[]{:S(2)}) async-start(f32[16,1,1,32]{3,2,1,0:T(1,128)} %copy.102), calls=%async_computation.1 | async-start | bytes 16384 | tf_op jit(solution)/shard_map/all_to_all | solution.py:111
  150.6 10.4 %all-to-all-start.3 = ((f32[16,1,1,32]{3,2,1,0:T(1,128)}), f32[16,1,1,32]{3,2,1,0:T(1,128)S(1)}, u32[]{:S(2)}, u32[]{:S(2)}) async-start(f32[16,1,1,32]{3,2,1,0:T(1,128)} %copy.107), calls=%async_computation.3 | async-start | bytes 16384 | tf_op jit(solution)/shard_map/all_to_all | solution.py:112
  161.0 23.7 %copy-start.6 = (f32[16,1,1,32]{3,2,1,0:T(1,128)}, f32[16,1,1,32]{3,2,1,0:T(1,128)S(1)}, u32[]{:S(2)}) copy-start(f32[16,1,1,32]{3,2,1,0:T(1,128)S(1)} %all-to-all-done.3) | copy-start | bytes 6148
  161.0 9.9 %all-to-all-start.4 = ((f32[16,1,1,32]{3,2,1,0:T(1,128)}), f32[16,1,1,32]{3,2,1,0:T(1,128)S(1)}, u32[]{:S(2)}, u32[]{:S(2)}) async-start(f32[16,1,1,32]{3,2,1,0:T(1,128)} %copy.108), calls=%async_computation.4 | async-start | bytes 16384 | tf_op jit(solution)/shard_map/all_to_all | solution.py:111
  170.9 9.8 %all-to-all-start.6 = ((f32[16,1,1,32]{3,2,1,0:T(1,128)}), f32[16,1,1,32]{3,2,1,0:T(1,128)S(1)}, u32[]{:S(2)}, u32[]{:S(2)}) async-start(f32[16,1,1,32]{3,2,1,0:T(1,128)} %copy.113), calls=%async_computation.6 | async-start | bytes 16384 | tf_op jit(solution)/shard_map/all_to_all | solution.py:112
  181.3 11.5 %all-to-all-start.7 = ((f32[16,1,1,32]{3,2,1,0:T(1,128)}), f32[16,1,1,32]{3,2,1,0:T(1,128)S(1)}, u32[]{:S(2)}, u32[]{:S(2)}) async-start(f32[16,1,1,32]{3,2,1,0:T(1,128)} %copy.114), calls=%async_computation.7 | async-start | bytes 16384 | tf_op jit(solution)/shard_map/all_to_all | solution.py:111
  192.7 12.3 %all-to-all-start.9 = ((f32[16,1,1,32]{3,2,1,0:T(1,128)}), f32[16,1,1,32]{3,2,1,0:T(1,128)S(1)}, u32[]{:S(2)}, u32[]{:S(2)}) async-start(f32[16,1,1,32]{3,2,1,0:T(1,128)} %copy.119), calls=%async_computation.9 | async-start | bytes 16384 | tf_op jit(solution)/shard_map/all_to_all | solution.py:112
  201.8 19.9 %copy-start.18 = (bf16[1,4,512]{2,1,0:T(4,128)(2,1)S(1)}, bf16[1,4,512]{2,1,0:T(4,128)(2,1)}, u32[]{:S(2)}) copy-start(bf16[1,4,512]{2,1,0:T(4,128)(2,1)} %param.22) | copy-start | bytes 12292
  201.8 20.3 %copy-start.7 = (f32[16,1,1,32]{3,2,1,0:T(1,128)S(1)}, f32[16,1,1,32]{3,2,1,0:T(1,128)}, u32[]{:S(2)}) copy-start(f32[16,1,1,32]{3,2,1,0:T(1,128)} %copy-done.6) | copy-start | bytes 6148
  201.8 20.3 %copy-start.9 = (f32[16,1,1,32]{3,2,1,0:T(1,128)S(1)}, f32[16,1,1,32]{3,2,1,0:T(1,128)}, u32[]{:S(2)}) copy-start(f32[16,1,1,32]{3,2,1,0:T(1,128)} %copy-done.8) | copy-start | bytes 6148
  205.7 9.9 %all-to-all-start.10 = ((f32[16,1,1,32]{3,2,1,0:T(1,128)}), f32[16,1,1,32]{3,2,1,0:T(1,128)S(1)}, u32[]{:S(2)}, u32[]{:S(2)}) async-start(f32[16,1,1,32]{3,2,1,0:T(1,128)} %copy.120), calls=%async_computation.10 | async-start | bytes 16384 | tf_op jit(solution)/shard_map/all_to_all | solution.py:111
  215.5 13.5 %all-to-all-start.2 = ((f32[16,1,1,4096]{3,1,2,0:T(1,128)}), f32[16,1,1,4096]{3,1,2,0:T(1,128)S(1)}, u32[]{:S(2)}, u32[]{:S(2)}) async-start(f32[16,1,1,4096]{3,1,2,0:T(1,128)} %bitcast.19), calls=%async_computation.2 | async-start | bytes 524288 | tf_op jit(solution)/shard_map/all_to_all | solution.py:110
  219.1 52.2 %copy-start.1 = (bf16[1920,512]{1,0:T(8,128)(2,1)S(1)}, bf16[1920,512]{1,0:T(8,128)(2,1)}, u32[]{:S(2)}) copy-start(bf16[1920,512]{1,0:T(8,128)(2,1)} %param.16) | copy-start | bytes 5898244
  229.1 13.5 %all-to-all-start.5 = ((f32[16,1,1,4096]{3,1,2,0:T(1,128)}), f32[16,1,1,4096]{3,1,2,0:T(1,128)S(1)}, u32[]{:S(2)}, u32[]{:S(2)}) async-start(f32[16,1,1,4096]{3,1,2,0:T(1,128)} %bitcast.35), calls=%async_computation.5 | async-start | bytes 524288 | tf_op jit(solution)/shard_map/all_to_all | solution.py:110
  242.6 13.5 %all-to-all-start.8 = ((f32[16,1,1,4096]{3,1,2,0:T(1,128)}), f32[16,1,1,4096]{3,1,2,0:T(1,128)S(1)}, u32[]{:S(2)}, u32[]{:S(2)}) async-start(f32[16,1,1,4096]{3,1,2,0:T(1,128)} %bitcast.50), calls=%async_computation.8 | async-start | bytes 524288 | tf_op jit(solution)/shard_map/all_to_all | solution.py:110
  256.2 13.5 %all-to-all-start.11 = ((f32[16,1,1,4096]{3,1,2,0:T(1,128)}), f32[16,1,1,4096]{3,1,2,0:T(1,128)S(1)}, u32[]{:S(2)}, u32[]{:S(2)}) async-start(f32[16,1,1,4096]{3,1,2,0:T(1,128)} %bitcast.65), calls=%async_computation.11 | async-start | bytes 524288 | tf_op jit(solution)/shard_map/all_to_all | solution.py:110
  (7 other events, 6.7 us)
where the time goes:
time: 273 us; the launch traced here: 271 us
  blocking collectives  83.6 us (31%)
  waiting for transfers between devices  59.9 us (22%)
  starting transfers between devices  45.6 us (17%)
  local copies, waits for them, and re-layouts  40.9 us (15%)
  other arithmetic  22.1 us (8%)
  matrix products  17.6 us (6%)
    all_gather x4, blocking collectives, prefix_attention(): whole = lax.all_gather(selected, 'seq', axis=0, tiled=True)  83.6 us
    all_to_all x4, waiting for transfers between devices, prefix_attention(): lax.all_to_all(parts[:, None], 'seq', split_axis=0, concat_axis=1, tiled=...  33.5 us
    all_to_all x4, starting transfers between devices, prefix_attention(): lax.all_to_all(totals[:, None], 'seq', split_axis=0, concat_axis=1, tiled...  17.2 us
    unnamed x61, local copies, waits for them, and re-layouts  14.6 us
    all_to_all x4, starting transfers between devices, prefix_attention(): lax.all_to_all(peaks[:, None], 'seq', split_axis=0, concat_axis=1, tiled=...  14.3 us
    all_to_all x4, starting transfers between devices, prefix_attention(): lax.all_to_all(parts[:, None], 'seq', split_axis=0, concat_axis=1, tiled=...  14.1 us
    another operation x2, local copies, waits for them, and re-layouts  13.9 us
    all_to_all x4, waiting for transfers between devices, prefix_attention(): lax.all_to_all(totals[:, None], 'seq', split_axis=0, concat_axis=1, tiled...  13.8 us
  transfers between devices with their start and end apart: 12, of which 10 were waited for; matrix products, arithmetic and copies ran while one was open for 17% of the time, Pallas kernels for 0%

commit v1 on v0

--- a/solution.py
+++ b/solution.py
@@ -98,7 +98,14 @@
 
     def prefix_attention(selected):
         width = selected.shape[1]
-        whole = lax.all_gather(selected, "seq", axis=0, tiled=True)
+        ring = [selected]
+        for hop in range(15):
+            ring.append(lax.ppermute(ring[-1], "seq", [(dev, (dev + 1) % 16) for dev in range(16)]))
+        whole = jnp.roll(
+            jnp.concatenate(ring[::-1], axis=0),
+            (lax.axis_index("seq") + 1) * ring[0].shape[0],
+            axis=0,
+        )
         count = whole.shape[0]
         per_block = math.gcd(count, max(1, 512 // (width * QH)))
         blocks = whole.reshape(count // per_block, per_block, width, QH * HD)

time: 273 us -> 260 us (0.952)
  blocking collectives: 83.6 us -> 0 us
  waiting for transfers between devices: 59.9 us -> 91.1 us
  starting transfers between devices: 45.6 us -> 71.7 us
  matrix products: 17.6 us -> 31.6 us
  local copies, waits for them, and re-layouts: 40.9 us -> 37.9 us
  other arithmetic: 22.1 us -> 24.9 us
    all_gather x4 -> x0, blocking collectives: 83.6 us -> none  [prefix_attention(): whole = lax.all_gather(selected, 'seq', axis=0, tiled=True)]
    ppermute x0 -> x60, waiting for transfers between devices: none -> 35.3 us  [prefix_attention(): lax.ppermute(ring[-1], 'seq', [(dev, (dev + 1) % 16) for dev in range(16)])]
    ppermute x0 -> x60, starting transfers between devices: none -> 27.3 us  [prefix_attention(): lax.ppermute(ring[-1], 'seq', [(dev, (dev + 1) % 16) for dev in range(16)])]
    dot_general x4, matrix products: 3.38 us -> 10.4 us  [shard_part(): jnp.einsum('rtkgp,pkd->rtkgd', expo.astype(jnp.bfloat16), values, preferr...]
    unnamed x61 -> x35, local copies, waits for them, and re-layouts: 14.6 us -> 10.1 us
    reduce_sum x4, other arithmetic: 3.1 us -> 7.33 us  [shard_part(): total = jnp.sum(expo, -1)]
    all_to_all x4, waiting for transfers between devices: 13.8 us -> 9.87 us  [prefix_attention(): lax.all_to_all(totals[:, None], 'seq', split_axis=0, concat_axis=1, tiled...]
    dot_general x4, matrix products: 3.18 us -> 6.76 us  [shard_part(): jnp.einsum('rtkgd,pkd->rtkgp', split, keys, preferred_element_type=jnp.fl...]
  transfers between devices with their start and end apart: 12 -> 72, of which waited for: 10 -> 42; matrix products, arithmetic and copies ran while one was open for 17% -> 34% of each run, Pallas kernels for 0% -> 0%
where the time goes in v1:
time: 260 us; the launch traced here: 259 us
  waiting for transfers between devices  91.1 us (35%)
  starting transfers between devices  71.7 us (28%)
  local copies, waits for them, and re-layouts  37.9 us (15%)
  matrix products  31.6 us (12%)
  other arithmetic  24.9 us (10%)
    ppermute x60, waiting for transfers between devices, prefix_attention(): lax.ppermute(ring[-1], 'seq', [(dev, (dev + 1) % 16) for dev in range(16)])  35.3 us
    all_to_all x4, waiting for transfers between devices, prefix_attention(): lax.all_to_all(parts[:, None], 'seq', split_axis=0, concat_axis=1, tiled=...  32.3 us
    ppermute x60, starting transfers between devices, prefix_attention(): lax.ppermute(ring[-1], 'seq', [(dev, (dev + 1) % 16) for dev in range(16)])  27.3 us
    all_to_all x4, starting transfers between devices, prefix_attention(): lax.all_to_all(totals[:, None], 'seq', split_axis=0, concat_axis=1, tiled...  15.3 us
    all_to_all x4, starting transfers between devices, prefix_attention(): lax.all_to_all(peaks[:, None], 'seq', split_axis=0, concat_axis=1, tiled=...  15.1 us
    all_to_all x4, starting transfers between devices, prefix_attention(): lax.all_to_all(parts[:, None], 'seq', split_axis=0, concat_axis=1, tiled=...  14.1 us
    another operation x2, local copies, waits for them, and re-layouts  13.8 us
    all_to_all x4, waiting for transfers between devices, prefix_attention(): lax.all_to_all(peaks[:, None], 'seq', split_axis=0, concat_axis=1, tiled=...  13.7 us
  transfers between devices with their start and end apart: 72, of which 42 were waited for; matrix products, arithmetic and copies ran while one was open for 34% of the time, Pallas kernels for 0%

profile of v1, /device:TPU:0, one launch (start us, length us, event | category | flops | bytes accessed | tf_op | source)
XLA Modules:
  0.0 258.7 jit_solution(16457712735561909151)
XLA Ops:
  13.9 5.6 %fusion.77 = (f32[1920,64]{1,0:T(8,128)S(1)}, f32[1920,64]{1,0:T(8,128)}) fusion(s32[64]{0:T(128)S(1)} %copy-done.9, s32[64]{0:T(128)S(1)} %copy-done.8, s32[1920]{0:T(1024)S(1)} %fusion.104), kind=kLoop, calls=%fused_computation.80 | loop fusion | flops 3440640 | bytes 991232 | tf_op jit(solution)/shard_map/cos | solution.py:31
  19.5 3.6 %copy.163 = f32[1920,4,64]{2,0,1:T(8,128)} copy(f32[1920,4,64]{0,2,1:T(8,128)} %get-tuple-element.73) | data formatting | bytes 3932160
  23.2 3.7 %copy.164 = f32[1920,4,64]{2,0,1:T(8,128)} copy(f32[1920,4,64]{0,2,1:T(8,128)} %get-tuple-element.72) | data formatting | bytes 3932160
  30.1 6.4 %subtract_convert_fusion = (bf16[1920,4,64]{2,0,1:T(8,128)(2,1)}, bf16[1920,4,64]{2,0,1:T(8,128)(2,1)}) fusion(f32[1920,4,64]{2,0,1:T(8,128)} %copy.164, f32[1920,4,64]{2,0,1:T(8,128)} %copy.163, f32[1920,64]{1,0:T(8,128)} %get-tuple-element.90, f32[1920,64]{1,0:T(8,128)S(1)} %get-tuple-element.89), kind=kLoop, calls=%fused_computation.20 | loop fusion | flops 3932160 | bytes 6881280 | tf_op jit(solution)/shard_map/convert.12
  39.8 6.9 %reshape.1695 = bf16[4096,4,128]{2,1,0:T(4,128)(2,1)} reshape(bf16[1,4096,512]{2,1,0:T(8,128)(2,1)} %param.25) | data formatting | bytes 8388608 | tf_op jit(solution)/shard_map/reshape.165
  48.7 5.1 %fusion.133 = (f32[4,4,8]{2,0,1:T(4,128)S(1)}, f32[1,4,4,8,4096]{4,3,1,2,0:T(8,128)}) fusion(bf16[4096,4,128,1]{2,1,0,3:T(4,128)(2,1)} %bitcast.298, pred[4096]{0:T(1024)(128)(4,1)S(1)} %iota_compare_fusion, bf16[4,4,8,64]{3,2,1,0:T(8,128)(2,1)S(1)} %bitcast.309, bf16[4,4,8,64]{3,2,1,0:T(8,128)(2,1)S(1)} %bitcast.307), kind=kOutput, calls=%fused_computation.183 | convolution fusion | flops 135856000 | bytes 6328832 | tf_op jit(solution)/shard_map/rtkgd,rpkd->rtkgp/dot_general | solution.py:138
  61.5 4.0 %collective-permute-done.35 = bf16[1,1,4096]{2,0,1:T(2,128)(2,1)S(1)} collective-permute-done((bf16[1,1,4096]{2,0,1:T(2,128)(2,1)S(1)}, bf16[1,1,4096]{2,0,1:T(2,128)(2,1)S(1)}, u32[]{:S(2)}, u32[]{:S(2)}) %collective-permute-start.35) | collective-permute-done | bytes 8224 | tf_op jit(solution)/shard_map/ppermute | solution.py:103
  67.3 4.0 %collective-permute-done.36 = bf16[1,1,4096]{2,0,1:T(2,128)(2,1)S(1)} collective-permute-done((bf16[1,1,4096]{2,0,1:T(2,128)(2,1)S(1)}, bf16[1,1,4096]{2,0,1:T(2,128)(2,1)S(1)}, u32[]{:S(2)}, u32[]{:S(2)}) %collective-permute-start.36) | collective-permute-done | bytes 8224 | tf_op jit(solution)/shard_map/ppermute | solution.py:103
  73.5 6.9 %reshape.1699 = bf16[4096,4,128]{2,1,0:T(4,128)(2,1)} reshape(bf16[1,4096,512]{2,1,0:T(8,128)(2,1)} %param.26) | data formatting | bytes 8388608 | tf_op jit(solution)/shard_map/reshape.180
  80.7 3.7 %fusion.3 = f32[4,4,8,128]{3,2,1,0:T(8,128)S(1)} fusion(bf16[4096,4,128,1]{2,1,0,3:T(4,128)(2,1)} %bitcast.297, f32[1,4,4,8,4096]{4,3,1,2,0:T(8,128)} %get-tuple-element.118, f32[4,4,8]{2,0,1:T(4,128)S(1)} %max.48), kind=kOutput, calls=%fused_computation.4 | convolution fusion | flops 135266304 | bytes 6357504 | tf_op jit(solution)/shard_map/rtkgp,rpkd->rtkgd/dot_general | solution.py:155
  93.0 3.9 %collective-permute-start.26 = (bf16[1,1,4096]{2,0,1:T(2,128)(2,1)S(1)}, bf16[1,1,4096]{2,0,1:T(2,128)(2,1)S(1)}, u32[]{:S(2)}, u32[]{:S(2)}) collective-permute-start(bf16[1,1,4096]{2,0,1:T(2,128)(2,1)S(1)} %collective-permute-done.25), channel_id=1, source_target_pairs={{0,1},{1,2},{2,3},{3,4},{4,5},{5,6},{6,7},{7,8},{8,9},{9,10},{10,1... | collective-permute-start | bytes 24584 | tf_op jit(solution)/shard_map/ppermute | solution.py:103
  106.0 3.8 %collective-permute-done.42 = bf16[1,1,4096]{2,0,1:T(2,128)(2,1)S(1)} collective-permute-done((bf16[1,1,4096]{2,0,1:T(2,128)(2,1)S(1)}, bf16[1,1,4096]{2,0,1:T(2,128)(2,1)S(1)}, u32[]{:S(2)}, u32[]{:S(2)}) %collective-permute-start.42) | collective-permute-done | bytes 8224 | tf_op jit(solution)/shard_map/ppermute | solution.py:103
  111.9 3.7 %collective-permute-done.43 = bf16[1,1,4096]{2,0,1:T(2,128)(2,1)S(1)} collective-permute-done((bf16[1,1,4096]{2,0,1:T(2,128)(2,1)S(1)}, bf16[1,1,4096]{2,0,1:T(2,128)(2,1)S(1)}, u32[]{:S(2)}, u32[]{:S(2)}) %collective-permute-start.43) | collective-permute-done | bytes 8224 | tf_op jit(solution)/shard_map/ppermute | solution.py:103
  122.2 4.6 %all-to-all-start = ((f32[16,1,1,32]{3,2,1,0:T(1,128)}), f32[16,1,1,32]{3,2,1,0:T(1,128)S(1)}, u32[]{:S(2)}, u32[]{:S(2)}) async-start(f32[16,1,1,32]{3,2,1,0:T(1,128)} %copy.106), calls=%async_computation | async-start | bytes 16384 | tf_op jit(solution)/shard_map/all_to_all | solution.py:119
  133.1 4.7 %all-to-all-start.1 = ((f32[16,1,1,32]{3,2,1,0:T(1,128)}), f32[16,1,1,32]{3,2,1,0:T(1,128)S(1)}, u32[]{:S(2)}, u32[]{:S(2)}) async-start(f32[16,1,1,32]{3,2,1,0:T(1,128)} %copy.107), calls=%async_computation.1 | async-start | bytes 16384 | tf_op jit(solution)/shard_map/all_to_all | solution.py:118
  138.7 5.5 %all-to-all-done.1 = f32[16,1,1,32]{3,2,1,0:T(1,128)S(1)} async-done(((f32[16,1,1,32]{3,2,1,0:T(1,128)}), f32[16,1,1,32]{3,2,1,0:T(1,128)S(1)}, u32[]{:S(2)}, u32[]{:S(2)}) %all-to-all-start.1) | async-done | bytes 2080 | tf_op jit(solution)/shard_map/all_to_all | solution.py:118
  144.2 3.7 %all-to-all-start.3 = ((f32[16,1,1,32]{3,2,1,0:T(1,128)}), f32[16,1,1,32]{3,2,1,0:T(1,128)S(1)}, u32[]{:S(2)}, u32[]{:S(2)}) async-start(f32[16,1,1,32]{3,2,1,0:T(1,128)} %copy.113), calls=%async_computation.3 | async-start | bytes 16384 | tf_op jit(solution)/shard_map/all_to_all | solution.py:119
  154.0 3.4 %all-to-all-start.4 = ((f32[16,1,1,32]{3,2,1,0:T(1,128)}), f32[16,1,1,32]{3,2,1,0:T(1,128)S(1)}, u32[]{:S(2)}, u32[]{:S(2)}) async-start(f32[16,1,1,32]{3,2,1,0:T(1,128)} %copy.114), calls=%async_computation.4 | async-start | bytes 16384 | tf_op jit(solution)/shard_map/all_to_all | solution.py:118
  163.8 3.5 %all-to-all-start.6 = ((f32[16,1,1,32]{3,2,1,0:T(1,128)}), f32[16,1,1,32]{3,2,1,0:T(1,128)S(1)}, u32[]{:S(2)}, u32[]{:S(2)}) async-start(f32[16,1,1,32]{3,2,1,0:T(1,128)} %copy.120), calls=%async_computation.6 | async-start | bytes 16384 | tf_op jit(solution)/shard_map/all_to_all | solution.py:119
  170.5 3.0 %all-to-all-done.6 = f32[16,1,1,32]{3,2,1,0:T(1,128)S(1)} async-done(((f32[16,1,1,32]{3,2,1,0:T(1,128)}), f32[16,1,1,32]{3,2,1,0:T(1,128)S(1)}, u32[]{:S(2)}, u32[]{:S(2)}) %all-to-all-start.6) | async-done | bytes 2080 | tf_op jit(solution)/shard_map/all_to_all | solution.py:119
  173.5 3.5 %all-to-all-start.7 = ((f32[16,1,1,32]{3,2,1,0:T(1,128)}), f32[16,1,1,32]{3,2,1,0:T(1,128)S(1)}, u32[]{:S(2)}, u32[]{:S(2)}) async-start(f32[16,1,1,32]{3,2,1,0:T(1,128)} %copy.121), calls=%async_computation.7 | async-start | bytes 16384 | tf_op jit(solution)/shard_map/all_to_all | solution.py:118
  183.4 3.5 %all-to-all-start.9 = ((f32[16,1,1,32]{3,2,1,0:T(1,128)}), f32[16,1,1,32]{3,2,1,0:T(1,128)S(1)}, u32[]{:S(2)}, u32[]{:S(2)}) async-start(f32[16,1,1,32]{3,2,1,0:T(1,128)} %copy.127), calls=%async_computation.9 | async-start | bytes 16384 | tf_op jit(solution)/shard_map/all_to_all | solution.py:119
  193.2 3.5 %all-to-all-start.10 = ((f32[16,1,1,32]{3,2,1,0:T(1,128)}), f32[16,1,1,32]{3,2,1,0:T(1,128)S(1)}, u32[]{:S(2)}, u32[]{:S(2)}) async-start(f32[16,1,1,32]{3,2,1,0:T(1,128)} %copy.128), calls=%async_computation.10 | async-start | bytes 16384 | tf_op jit(solution)/shard_map/all_to_all | solution.py:118
  203.0 3.5 %all-to-all-start.2 = ((f32[16,1,1,4096]{3,1,2,0:T(1,128)}), f32[16,1,1,4096]{3,1,2,0:T(1,128)S(1)}, u32[]{:S(2)}, u32[]{:S(2)}) async-start(f32[16,1,1,4096]{3,1,2,0:T(1,128)} %bitcast.19), calls=%async_computation.2 | async-start | bytes 524288 | tf_op jit(solution)/shard_map/all_to_all | solution.py:117
  206.6 3.7 %fusion.55 = f32[16,1,4,8,128]{4,0,3,2,1:T(8,128)S(1)} fusion(bf16[1920,4,128,1]{0,2,3,1:T(8,128)(2,1)} %bitcast.351, f32[4,1920,16,8]{1,2,3,0:T(8,128)} %get-tuple-element.101, f32[16,4,8]{0,2,1:T(8,128)S(1)} %get-tuple-element.100, f32[16,4,8]{0,2,1:T(8,128)S(1)} %fusion.17), kind=kOutput, calls=%fused_computation.67 | convolution fusion | flops 254672896 | bytes 6164480 | tf_op jit(solution)/shard_map/while/body/eval_jaxpr/rtkgp,pkd->rtkgd/dot_general | solution.py:86
  212.8 3.7 %all-to-all-done.2 = f32[16,1,1,4096]{3,1,2,0:T(1,128)S(1)} async-done(((f32[16,1,1,4096]{3,1,2,0:T(1,128)}), f32[16,1,1,4096]{3,1,2,0:T(1,128)S(1)}, u32[]{:S(2)}, u32[]{:S(2)}) %all-to-all-start.2) | async-done | bytes 262176 | tf_op jit(solution)/shard_map/all_to_all | solution.py:117
  216.6 3.5 %all-to-all-start.5 = ((f32[16,1,1,4096]{3,1,2,0:T(1,128)}), f32[16,1,1,4096]{3,1,2,0:T(1,128)S(1)}, u32[]{:S(2)}, u32[]{:S(2)}) async-start(f32[16,1,1,4096]{3,1,2,0:T(1,128)} %bitcast.35), calls=%async_computation.5 | async-start | bytes 524288 | tf_op jit(solution)/shard_map/all_to_all | solution.py:117
  220.2 10.0 %all-to-all-done.5 = f32[16,1,1,4096]{3,1,2,0:T(1,128)S(1)} async-done(((f32[16,1,1,4096]{3,1,2,0:T(1,128)}), f32[16,1,1,4096]{3,1,2,0:T(1,128)S(1)}, u32[]{:S(2)}, u32[]{:S(2)}) %all-to-all-start.5) | async-done | bytes 262176 | tf_op jit(solution)/shard_map/all_to_all | solution.py:117
  230.1 3.5 %all-to-all-start.8 = ((f32[16,1,1,4096]{3,1,2,0:T(1,128)}), f32[16,1,1,4096]{3,1,2,0:T(1,128)S(1)}, u32[]{:S(2)}, u32[]{:S(2)}) async-start(f32[16,1,1,4096]{3,1,2,0:T(1,128)} %bitcast.50), calls=%async_computation.8 | async-start | bytes 524288 | tf_op jit(solution)/shard_map/all_to_all | solution.py:117
  233.7 9.9 %all-to-all-done.8 = f32[16,1,1,4096]{3,1,2,0:T(1,128)S(1)} async-done(((f32[16,1,1,4096]{3,1,2,0:T(1,128)}), f32[16,1,1,4096]{3,1,2,0:T(1,128)S(1)}, u32[]{:S(2)}, u32[]{:S(2)}) %all-to-all-start.8) | async-done | bytes 262176 | tf_op jit(solution)/shard_map/all_to_all | solution.py:117
  243.7 3.5 %all-to-all-start.11 = ((f32[16,1,1,4096]{3,1,2,0:T(1,128)}), f32[16,1,1,4096]{3,1,2,0:T(1,128)S(1)}, u32[]{:S(2)}, u32[]{:S(2)}) async-start(f32[16,1,1,4096]{3,1,2,0:T(1,128)} %bitcast.65), calls=%async_computation.11 | async-start | bytes 524288 | tf_op jit(solution)/shard_map/all_to_all | solution.py:117
  248.5 8.7 %all-to-all-done.11 = f32[16,1,1,4096]{3,1,2,0:T(1,128)S(1)} async-done(((f32[16,1,1,4096]{3,1,2,0:T(1,128)}), f32[16,1,1,4096]{3,1,2,0:T(1,128)S(1)}, u32[]{:S(2)}, u32[]{:S(2)}) %all-to-all-start.11) | async-done | bytes 262176 | tf_op jit(solution)/shard_map/all_to_all | solution.py:117
  (237 shorter events, 106.9 us)
Async XLA Ops:
  2.7 9.6 %collective-permute-start = (bf16[1,1,4096]{2,0,1:T(2,128)(2,1)S(1)}, bf16[1,1,4096]{2,0,1:T(2,128)(2,1)S(1)}, u32[]{:S(2)}, u32[]{:S(2)}) collective-permute-start(bf16[1,1,4096]{2,0,1:T(2,128)(2,1)S(1)} %get-tuple-element.76), channel_id=1, source_target_pairs={{0,1},{1,2},{2,3},{3,4},{4,5},{5,6},{6,7},{7,8},{8,9},{9,10},{10,1... | collective-permute-start | bytes 24584 | tf_op jit(solution)/shard_map/ppermute | solution.py:103
  3.2 9.1 %collective-permute-start.15 = (bf16[1,1,4096]{2,0,1:T(2,128)(2,1)S(1)}, bf16[1,1,4096]{2,0,1:T(2,128)(2,1)S(1)}, u32[]{:S(2)}, u32[]{:S(2)}) collective-permute-start(bf16[1,1,4096]{2,0,1:T(2,128)(2,1)S(1)} %get-tuple-element.86), channel_id=1, source_target_pairs={{0,1},{1,2},{2,3},{3,4},{4,5},{5,6},{6,7},{7,8},{8,9},{9,10},{10,1... | collective-permute-start | bytes 24584 | tf_op jit(solution)/shard_map/ppermute | solution.py:103
  5.8 21.0 %collective-permute-start.30 = (bf16[1,1,4096]{2,0,1:T(2,128)(2,1)S(1)}, bf16[1,1,4096]{2,0,1:T(2,128)(2,1)S(1)}, u32[]{:S(2)}, u32[]{:S(2)}) collective-permute-start(bf16[1,1,4096]{2,0,1:T(2,128)(2,1)S(1)} %get-tuple-element.85), channel_id=1, source_target_pairs={{0,1},{1,2},{2,3},{3,4},{4,5},{5,6},{6,7},{7,8},{8,9},{9,10},{10,1... | collective-permute-start | bytes 24584 | tf_op jit(solution)/shard_map/ppermute | solution.py:103
  5.9 21.0 %collective-permute-start.45 = (bf16[1,1,4096]{2,0,1:T(2,128)(2,1)S(1)}, bf16[1,1,4096]{2,0,1:T(2,128)(2,1)S(1)}, u32[]{:S(2)}, u32[]{:S(2)}) collective-permute-start(bf16[1,1,4096]{2,0,1:T(2,128)(2,1)S(1)} %get-tuple-element.84), channel_id=1, source_target_pairs={{0,1},{1,2},{2,3},{3,4},{4,5},{5,6},{6,7},{7,8},{8,9},{9,10},{10,1... | collective-permute-start | bytes 24584 | tf_op jit(solution)/shard_map/ppermute | solution.py:103
  12.3 16.2 %collective-permute-start.1 = (bf16[1,1,4096]{2,0,1:T(2,128)(2,1)S(1)}, bf16[1,1,4096]{2,0,1:T(2,128)(2,1)S(1)}, u32[]{:S(2)}, u32[]{:S(2)}) collective-permute-start(bf16[1,1,4096]{2,0,1:T(2,128)(2,1)S(1)} %collective-permute-done), channel_id=1, source_target_pairs={{0,1},{1,2},{2,3},{3,4},{4,5},{5,6},{6,7},{7,8},{8,9},{9,10},{10,1... | collective-permute-start | bytes 24584 | tf_op jit(solution)/shard_map/ppermute | solution.py:103
  12.3 16.2 %collective-permute-start.16 = (bf16[1,1,4096]{2,0,1:T(2,128)(2,1)S(1)}, bf16[1,1,4096]{2,0,1:T(2,128)(2,1)S(1)}, u32[]{:S(2)}, u32[]{:S(2)}) collective-permute-start(bf16[1,1,4096]{2,0,1:T(2,128)(2,1)S(1)} %collective-permute-done.15), channel_id=1, source_target_pairs={{0,1},{1,2},{2,3},{3,4},{4,5},{5,6},{6,7},{7,8},{8,9},{9,10},{10,1... | collective-permute-start | bytes 24584 | tf_op jit(solution)/shard_map/ppermute | solution.py:103
  26.8 9.7 %collective-permute-start.31 = (bf16[1,1,4096]{2,0,1:T(2,128)(2,1)S(1)}, bf16[1,1,4096]{2,0,1:T(2,128)(2,1)S(1)}, u32[]{:S(2)}, u32[]{:S(2)}) collective-permute-start(bf16[1,1,4096]{2,0,1:T(2,128)(2,1)S(1)} %collective-permute-done.30), channel_id=1, source_target_pairs={{0,1},{1,2},{2,3},{3,4},{4,5},{5,6},{6,7},{7,8},{8,9},{9,10},{10,1... | collective-permute-start | bytes 24584 | tf_op jit(solution)/shard_map/ppermute | solution.py:103
  26.9 9.7 %collective-permute-start.46 = (bf16[1,1,4096]{2,0,1:T(2,128)(2,1)S(1)}, bf16[1,1,4096]{2,0,1:T(2,128)(2,1)S(1)}, u32[]{:S(2)}, u32[]{:S(2)}) collective-permute-start(bf16[1,1,4096]{2,0,1:T(2,128)(2,1)S(1)} %collective-permute-done.45), channel_id=1, source_target_pairs={{0,1},{1,2},{2,3},{3,4},{4,5},{5,6},{6,7},{7,8},{8,9},{9,10},{10,1... | collective-permute-start | bytes 24584 | tf_op jit(solution)/shard_map/ppermute | solution.py:103
  28.5 9.7 %collective-permute-start.2 = (bf16[1,1,4096]{2,0,1:T(2,128)(2,1)S(1)}, bf16[1,1,4096]{2,0,1:T(2,128)(2,1)S(1)}, u32[]{:S(2)}, u32[]{:S(2)}) collective-permute-start(bf16[1,1,4096]{2,0,1:T(2,128)(2,1)S(1)} %collective-permute-done.1), channel_id=1, source_target_pairs={{0,1},{1,2},{2,3},{3,4},{4,5},{5,6},{6,7},{7,8},{8,9},{9,10},{10,1... | collective-permute-start | bytes 24584 | tf_op jit(solution)/shard_map/ppermute | solution.py:103
  28.6 9.7 %collective-permute-start.17 = (bf16[1,1,4096]{2,0,1:T(2,128)(2,1)S(1)}, bf16[1,1,4096]{2,0,1:T(2,128)(2,1)S(1)}, u32[]{:S(2)}, u32[]{:S(2)}) collective-permute-start(bf16[1,1,4096]{2,0,1:T(2,128)(2,1)S(1)} %collective-permute-done.16), channel_id=1, source_target_pairs={{0,1},{1,2},{2,3},{3,4},{4,5},{5,6},{6,7},{7,8},{8,9},{9,10},{10,1... | collective-permute-start | bytes 24584 | tf_op jit(solution)/shard_map/ppermute | solution.py:103
  36.5 10.2 %collective-permute-start.32 = (bf16[1,1,4096]{2,0,1:T(2,128)(2,1)S(1)}, bf16[1,1,4096]{2,0,1:T(2,128)(2,1)S(1)}, u32[]{:S(2)}, u32[]{:S(2)}) collective-permute-start(bf16[1,1,4096]{2,0,1:T(2,128)(2,1)S(1)} %collective-permute-done.31), channel_id=1, source_target_pairs={{0,1},{1,2},{2,3},{3,4},{4,5},{5,6},{6,7},{7,8},{8,9},{9,10},{10,1... | collective-permute-start | bytes 24584 | tf_op jit(solution)/shard_map/ppermute | solution.py:103
  36.6 10.2 %collective-permute-start.47 = (bf16[1,1,4096]{2,0,1:T(2,128)(2,1)S(1)}, bf16[1,1,4096]{2,0,1:T(2,128)(2,1)S(1)}, u32[]{:S(2)}, u32[]{:S(2)}) collective-permute-start(bf16[1,1,4096]{2,0,1:T(2,128)(2,1)S(1)} %collective-permute-done.46), channel_id=1, source_target_pairs={{0,1},{1,2},{2,3},{3,4},{4,5},{5,6},{6,7},{7,8},{8,9},{9,10},{10,1... | collective-permute-start | bytes 24584 | tf_op jit(solution)/shard_map/ppermute | solution.py:103
  38.2 8.7 %collective-permute-start.3 = (bf16[1,1,4096]{2,0,1:T(2,128)(2,1)S(1)}, bf16[1,1,4096]{2,0,1:T(2,128)(2,1)S(1)}, u32[]{:S(2)}, u32[]{:S(2)}) collective-permute-start(bf16[1,1,4096]{2,0,1:T(2,128)(2,1)S(1)} %collective-permute-done.2), channel_id=1, source_target_pairs={{0,1},{1,2},{2,3},{3,4},{4,5},{5,6},{6,7},{7,8},{8,9},{9,10},{10,1... | collective-permute-start | bytes 24584 | tf_op jit(solution)/shard_map/ppermute | solution.py:103
  38.2 8.7 %collective-permute-start.18 = (bf16[1,1,4096]{2,0,1:T(2,128)(2,1)S(1)}, bf16[1,1,4096]{2,0,1:T(2,128)(2,1)S(1)}, u32[]{:S(2)}, u32[]{:S(2)}) collective-permute-start(bf16[1,1,4096]{2,0,1:T(2,128)(2,1)S(1)} %collective-permute-done.17), channel_id=1, source_target_pairs={{0,1},{1,2},{2,3},{3,4},{4,5},{5,6},{6,7},{7,8},{8,9},{9,10},{10,1... | collective-permute-start | bytes 24584 | tf_op jit(solution)/shard_map/ppermute | solution.py:103
  46.9 8.5 %collective-permute-start.4 = (bf16[1,1,4096]{2,0,1:T(2,128)(2,1)S(1)}, bf16[1,1,4096]{2,0,1:T(2,128)(2,1)S(1)}, u32[]{:S(2)}, u32[]{:S(2)}) collective-permute-start(bf16[1,1,4096]{2,0,1:T(2,128)(2,1)S(1)} %collective-permute-done.3), channel_id=1, source_target_pairs={{0,1},{1,2},{2,3},{3,4},{4,5},{5,6},{6,7},{7,8},{8,9},{9,10},{10,1... | collective-permute-start | bytes 24584 | tf_op jit(solution)/shard_map/ppermute | solution.py:103
  46.9 8.5 %collective-permute-start.19 = (bf16[1,1,4096]{2,0,1:T(2,128)(2,1)S(1)}, bf16[1,1,4096]{2,0,1:T(2,128)(2,1)S(1)}, u32[]{:S(2)}, u32[]{:S(2)}) collective-permute-start(bf16[1,1,4096]{2,0,1:T(2,128)(2,1)S(1)} %collective-permute-done.18), channel_id=1, source_target_pairs={{0,1},{1,2},{2,3},{3,4},{4,5},{5,6},{6,7},{7,8},{8,9},{9,10},{10,1... | collective-permute-start | bytes 24584 | tf_op jit(solution)/shard_map/ppermute | solution.py:103
  71.4 9.1 %collective-permute-start.37 = (bf16[1,1,4096]{2,0,1:T(2,128)(2,1)S(1)}, bf16[1,1,4096]{2,0,1:T(2,128)(2,1)S(1)}, u32[]{:S(2)}, u32[]{:S(2)}) collective-permute-start(bf16[1,1,4096]{2,0,1:T(2,128)(2,1)S(1)} %collective-permute-done.36), channel_id=1, source_target_pairs={{0,1},{1,2},{2,3},{3,4},{4,5},{5,6},{6,7},{7,8},{8,9},{9,10},{10,1... | collective-permute-start | bytes 24584 | tf_op jit(solution)/shard_map/ppermute | solution.py:103
  71.5 9.0 %collective-permute-start.52 = (bf16[1,1,4096]{2,0,1:T(2,128)(2,1)S(1)}, bf16[1,1,4096]{2,0,1:T(2,128)(2,1)S(1)}, u32[]{:S(2)}, u32[]{:S(2)}) collective-permute-start(bf16[1,1,4096]{2,0,1:T(2,128)(2,1)S(1)} %collective-permute-done.51), channel_id=1, source_target_pairs={{0,1},{1,2},{2,3},{3,4},{4,5},{5,6},{6,7},{7,8},{8,9},{9,10},{10,1... | collective-permute-start | bytes 24584 | tf_op jit(solution)/shard_map/ppermute | solution.py:103
  115.7 15.3 %collective-permute-start.44 = (bf16[1,1,4096]{2,0,1:T(2,128)(2,1)S(1)}, bf16[1,1,4096]{2,0,1:T(2,128)(2,1)S(1)}, u32[]{:S(2)}, u32[]{:S(2)}) collective-permute-start(bf16[1,1,4096]{2,0,1:T(2,128)(2,1)S(1)} %collective-permute-done.43), channel_id=1, source_target_pairs={{0,1},{1,2},{2,3},{3,4},{4,5},{5,6},{6,7},{7,8},{8,9},{9,10},{10,1... | collective-permute-start | bytes 24584 | tf_op jit(solution)/shard_map/ppermute | solution.py:103
  115.9 15.5 %collective-permute-start.59 = (bf16[1,1,4096]{2,0,1:T(2,128)(2,1)S(1)}, bf16[1,1,4096]{2,0,1:T(2,128)(2,1)S(1)}, u32[]{:S(2)}, u32[]{:S(2)}) collective-permute-start(bf16[1,1,4096]{2,0,1:T(2,128)(2,1)S(1)} %collective-permute-done.58), channel_id=1, source_target_pairs={{0,1},{1,2},{2,3},{3,4},{4,5},{5,6},{6,7},{7,8},{8,9},{9,10},{10,1... | collective-permute-start | bytes 24584 | tf_op jit(solution)/shard_map/ppermute | solution.py:103
  122.2 11.0 %all-to-all-start = ((f32[16,1,1,32]{3,2,1,0:T(1,128)}), f32[16,1,1,32]{3,2,1,0:T(1,128)S(1)}, u32[]{:S(2)}, u32[]{:S(2)}) async-start(f32[16,1,1,32]{3,2,1,0:T(1,128)} %copy.106), calls=%async_computation | async-start | bytes 16384 | tf_op jit(solution)/shard_map/all_to_all | solution.py:119
  133.1 11.1 %all-to-all-start.1 = ((f32[16,1,1,32]{3,2,1,0:T(1,128)}), f32[16,1,1,32]{3,2,1,0:T(1,128)S(1)}, u32[]{:S(2)}, u32[]{:S(2)}) async-start(f32[16,1,1,32]{3,2,1,0:T(1,128)} %copy.107), calls=%async_computation.1 | async-start | bytes 16384 | tf_op jit(solution)/shard_map/all_to_all | solution.py:118
  144.2 9.8 %all-to-all-start.3 = ((f32[16,1,1,32]{3,2,1,0:T(1,128)}), f32[16,1,1,32]{3,2,1,0:T(1,128)S(1)}, u32[]{:S(2)}, u32[]{:S(2)}) async-start(f32[16,1,1,32]{3,2,1,0:T(1,128)} %copy.113), calls=%async_computation.3 | async-start | bytes 16384 | tf_op jit(solution)/shard_map/all_to_all | solution.py:119
  154.0 9.8 %all-to-all-start.4 = ((f32[16,1,1,32]{3,2,1,0:T(1,128)}), f32[16,1,1,32]{3,2,1,0:T(1,128)S(1)}, u32[]{:S(2)}, u32[]{:S(2)}) async-start(f32[16,1,1,32]{3,2,1,0:T(1,128)} %copy.114), calls=%async_computation.4 | async-start | bytes 16384 | tf_op jit(solution)/shard_map/all_to_all | solution.py:118
  163.8 9.8 %all-to-all-start.6 = ((f32[16,1,1,32]{3,2,1,0:T(1,128)}), f32[16,1,1,32]{3,2,1,0:T(1,128)S(1)}, u32[]{:S(2)}, u32[]{:S(2)}) async-start(f32[16,1,1,32]{3,2,1,0:T(1,128)} %copy.120), calls=%async_computation.6 | async-start | bytes 16384 | tf_op jit(solution)/shard_map/all_to_all | solution.py:119
  173.5 9.9 %all-to-all-start.7 = ((f32[16,1,1,32]{3,2,1,0:T(1,128)}), f32[16,1,1,32]{3,2,1,0:T(1,128)S(1)}, u32[]{:S(2)}, u32[]{:S(2)}) async-start(f32[16,1,1,32]{3,2,1,0:T(1,128)} %copy.121), calls=%async_computation.7 | async-start | bytes 16384 | tf_op jit(solution)/shard_map/all_to_all | solution.py:118
  183.4 9.8 %all-to-all-start.9 = ((f32[16,1,1,32]{3,2,1,0:T(1,128)}), f32[16,1,1,32]{3,2,1,0:T(1,128)S(1)}, u32[]{:S(2)}, u32[]{:S(2)}) async-start(f32[16,1,1,32]{3,2,1,0:T(1,128)} %copy.127), calls=%async_computation.9 | async-start | bytes 16384 | tf_op jit(solution)/shard_map/all_to_all | solution.py:119
  193.2 9.9 %all-to-all-start.10 = ((f32[16,1,1,32]{3,2,1,0:T(1,128)}), f32[16,1,1,32]{3,2,1,0:T(1,128)S(1)}, u32[]{:S(2)}, u32[]{:S(2)}) async-start(f32[16,1,1,32]{3,2,1,0:T(1,128)} %copy.128), calls=%async_computation.10 | async-start | bytes 16384 | tf_op jit(solution)/shard_map/all_to_all | solution.py:118
  203.0 13.5 %all-to-all-start.2 = ((f32[16,1,1,4096]{3,1,2,0:T(1,128)}), f32[16,1,1,4096]{3,1,2,0:T(1,128)S(1)}, u32[]{:S(2)}, u32[]{:S(2)}) async-start(f32[16,1,1,4096]{3,1,2,0:T(1,128)} %bitcast.19), calls=%async_computation.2 | async-start | bytes 524288 | tf_op jit(solution)/shard_map/all_to_all | solution.py:117
  216.6 13.5 %all-to-all-start.5 = ((f32[16,1,1,4096]{3,1,2,0:T(1,128)}), f32[16,1,1,4096]{3,1,2,0:T(1,128)S(1)}, u32[]{:S(2)}, u32[]{:S(2)}) async-start(f32[16,1,1,4096]{3,1,2,0:T(1,128)} %bitcast.35), calls=%async_computation.5 | async-start | bytes 524288 | tf_op jit(solution)/shard_map/all_to_all | solution.py:117
  230.1 13.5 %all-to-all-start.8 = ((f32[16,1,1,4096]{3,1,2,0:T(1,128)}), f32[16,1,1,4096]{3,1,2,0:T(1,128)S(1)}, u32[]{:S(2)}, u32[]{:S(2)}) async-start(f32[16,1,1,4096]{3,1,2,0:T(1,128)} %bitcast.50), calls=%async_computation.8 | async-start | bytes 524288 | tf_op jit(solution)/shard_map/all_to_all | solution.py:117
  243.7 13.5 %all-to-all-start.11 = ((f32[16,1,1,4096]{3,1,2,0:T(1,128)}), f32[16,1,1,4096]{3,1,2,0:T(1,128)S(1)}, u32[]{:S(2)}, u32[]{:S(2)}) async-start(f32[16,1,1,4096]{3,1,2,0:T(1,128)} %bitcast.65), calls=%async_computation.11 | async-start | bytes 524288 | tf_op jit(solution)/shard_map/all_to_all | solution.py:117
  (54 other events, 396.5 us)
